TPU v7x, 256 devices: a whole 4x4x8 slice. The times are simulated.
256 devices in a mesh: mode: 16 (over z_hi, y), gz: 16 (over z_lo, x, core).
Axes of the slice: x: 4, y: 4, z: 8 (z_hi: 4, z_lo: 2; z = z_hi * 2 + z_lo), core: 2. Of those that a mesh axis runs over, the one named last changes fastest.
Arguments:
- efield: float32 [3, 256, 256, 256], P(None, 'mode', 'gz'), may hold values from -0.6 to 0.6
- hfield: float32 [3, 256, 256, 256], P(None, 'mode', 'gz'), may hold values from -0.6 to 0.6
- polar: float32 [3, 16, 16, 256, 512], P(None, 'gz', 'mode'), may hold values from -1.2 to 1.2
- velocity: float32 [3, 16, 16, 256, 512], P(None, 'gz', 'mode'), may hold values from -0.5 to 0.5
- material: float32 [4, 16, 16, 256], P(None, 'gz', 'mode'), may hold values from 0.05 to 0.5
Outputs:
- new_efield: float32 [3, 256, 256, 256], P(None, 'mode', 'gz')
- new_hfield: float32 [3, 256, 256, 256], P(None, 'mode', 'gz')
- new_polar: float32 [3, 16, 16, 256, 512], P(None, 'gz', 'mode')
- new_velocity: float32 [3, 16, 16, 256, 512], P(None, 'gz', 'mode')
All inputs are finite; a program needn't handle non-finite values.
Results may differ from a plain program's by a relative error of at most 0.0001.
Values sent between devices are 32-bit elements; how exact they have to be, the bound alone decides.
A program may use at most 64 MiB of HBM per device.

v0:
```python
import jax
import jax.numpy as jnp
import ml_dtypes
import numpy as np
from jax import lax
from jax.experimental import pallas as pl
from jax.experimental.pallas import tpu as pltpu
from jax.sharding import PartitionSpec as P

M = 256
R = 256
NA = 512
SUBSTEPS = 4
G = 16
OWN = 16
TIME_STEP = 0.7 / M
RATIO = 0.5
MESH = pl.DeviceIdType.MESH
F32 = jnp.float32
BF16 = jnp.bfloat16


def tables():
    k = np.arange(M)
    phase = (k // 2)[:, None] * np.arange(NA)[None, :] % NA
    theta = 2.0 * np.pi * phase / NA
    basis = np.where((k % 2)[:, None] == 0, np.cos(theta), np.sin(theta))
    high = basis.astype(ml_dtypes.bfloat16)
    low = (basis - high.astype(np.float64)).astype(ml_dtypes.bfloat16)
    return np.stack([high, low])


def split(value):
    high = value.astype(BF16)
    return high, (value - high.astype(F32)).astype(BF16)


def dot3(a, b, dims):
    mul = lambda x, y: lax.dot_general(x, y, (dims, ((), ())), preferred_element_type=F32)
    return mul(a[0], b[0]) + (mul(a[1], b[0]) + mul(a[0], b[1]))


def shift_lanes(value, amount, keep):
    return jnp.where(keep, pltpu.roll(value, amount % value.shape[1], 1), 0.0)


def kernel(
    e_in, h_in, p_in, v_in, mat_in, tab_in,
    e_out, h_out, p_out, v_out,
    e0, h0, h1, x1, e1, h2, x2, c1, c2, f1, f2, ch1, ch2,
    pol, vel, pts, mat, coef, tab, below1, above1, below2, above2,
    load_sem, send_sem, recv_sem, own_sem, halo_send, halo_recv, out_sem,
):
    me = lax.axis_index("mode")
    gz = lax.axis_index("gz")
    zh, y = me // 4, lax.rem(me, 4)
    up, down = lax.rem(gz + 1, G), lax.rem(gz + G - 1, G)

    def each(fn):
        for dz in range(4):
            def body(dy, carry, dz=dz):
                fn(dz * 4 + dy, lax.rem(zh + dz, 4) * 4 + lax.rem(y + dy, 4))
                return carry
            lax.fori_loop(1 if dz == 0 else 0, 4, body, 0)

    loads = [
        pltpu.make_async_copy(s, d, load_sem.at[i])
        for i, (s, d) in enumerate(
            [(e_in, e0), (h_in, h0), (p_in, pol), (v_in, vel), (mat_in, mat), (tab_in, tab)]
        )
    ]
    for copy in loads:
        copy.start()

    barrier = pltpu.get_barrier_semaphore()
    each(lambda i, p: pl.semaphore_signal(barrier, 1, device_id={"mode": p}, device_id_type=MESH))
    pl.semaphore_signal(barrier, 1, device_id={"gz": up}, device_id_type=MESH)
    pl.semaphore_signal(barrier, 1, device_id={"gz": down}, device_id_type=MESH)
    pl.semaphore_wait(barrier, OWN + 1)

    def exchange(stage, source, target):
        def make(i, p):
            return pltpu.make_async_remote_copy(
                source(p), target, send_sem.at[stage, i], recv_sem.at[stage, i],
                device_id={"mode": p}, device_id_type=MESH,
            )
        own = pltpu.make_async_copy(source(me), target, own_sem.at[stage])

        def start():
            each(lambda i, p: make(i, p).start())
            own.start()

        def wait_recv():
            each(lambda i, p: make(i, p).wait_recv())
            own.wait()

        def wait_send():
            each(lambda i, p: make(i, p).wait_send())

        return start, wait_recv, wait_send

    mine = pl.ds(pl.multiple_of(me * OWN, OWN), OWN)
    rows = lambda p: pl.ds(pl.multiple_of(p * OWN, OWN), OWN)
    go1 = exchange(0, lambda p: e_in.at[:, :, p, :], f1.at[:, mine, :])
    go2 = exchange(1, lambda p: x1.at[:, :, p, :], f2.at[:, mine, :])
    back1 = exchange(2, lambda p: ch1.at[:, rows(p), :], c1.at[:, :, me, :])
    back2 = exchange(3, lambda p: ch2.at[:, rows(p), :], c2.at[:, :, me, :])

    def halo(stage, e, h, below, above):
        def make(i, source, target, to):
            return pltpu.make_async_remote_copy(
                source, target, halo_send.at[stage, i], halo_recv.at[stage, i],
                device_id={"gz": to}, device_id_type=MESH,
            )
        return [
            make(0, e.at[:, :, OWN - 1, :], below.at[0:3], up),
            make(1, h.at[0:2, :, OWN - 1, :], below.at[3:5], up),
            make(2, e.at[0:2, :, 0, :], above, down),
        ]

    go1[0]()
    loads[0].wait()
    loads[1].wait()
    halo1 = halo(0, e0, h0, below1, above1)
    halo2 = halo(1, e1, h1, below2, above2)
    for copy in halo1:
        copy.start()

    lane = lax.broadcasted_iota(jnp.int32, (1, R), 1)
    outer = lane.astype(F32) + 1.0
    inner = lane.astype(F32) + 0.5
    per_outer, per_inner = TIME_STEP / outer, TIME_STEP / inner
    keep_down, keep_up = lane > 0, lane < R - 1
    plane = lax.broadcasted_iota(jnp.int32, (OWN, 1), 0)

    down_r = lambda f: f - shift_lanes(f, 1, keep_down)
    up_r = lambda f: shift_lanes(f, -1, keep_up) - f
    up_z = lambda f, row: jnp.where(plane == OWN - 1, row, pltpu.roll(f, OWN - 1, 0)) - f
    down_z = lambda f, row: f - jnp.where(plane == 0, row, pltpu.roll(f, 1, 0))

    def maxwell(e, h, below, above, h_new, e_new):
        def pair(a, carry):
            order = (me * (OWN // 2) + a).astype(F32)
            signed = (order, -order)
            er, ef, ez, hr, hf, hz = (
                [f[c, 2 * a + s] for s in range(2)] for f in (e, h) for c in range(3)
            )
            ber, bef, bez, bhr, bhf = (
                [below[c, pl.ds(2 * a + s, 1), :] for s in range(2)] for c in range(5)
            )
            edge = lambda c, s: jnp.where(gz == G - 1, 0.0, above[c, pl.ds(2 * a + s, 1), :])
            nr, nf, nz, lr, lf = [], [], [], [], []
            for s in range(2):
                t = 1 - s
                nr.append(hr[s] - (signed[s] * ez[t]) * per_outer + RATIO * up_z(ef[s], edge(1, s)))
                nf.append(hf[s] - RATIO * up_z(er[s], edge(0, s)) + TIME_STEP * down_r(ez[s]))
                nz.append(hz[s] - (down_r(outer * ef[s]) - signed[s] * er[t]) * per_inner)
                r = bhr[s] - (signed[s] * bez[t]) * per_outer + RATIO * (ef[s][0:1] - bef[s])
                f = bhf[s] - RATIO * (er[s][0:1] - ber[s]) + TIME_STEP * down_r(bez[s])
                lr.append(jnp.where(gz == 0, 0.0, r))
                lf.append(jnp.where(gz == 0, 0.0, f))
            for s in range(2):
                t = 1 - s
                k = 2 * a + s
                h_new[0, k], h_new[1, k], h_new[2, k] = nr[s], nf[s], nz[s]
                e_new[0, k] = er[s] + (signed[s] * nz[t]) * per_inner - RATIO * down_z(nf[s], lf[s])
                e_new[1, k] = ef[s] + RATIO * down_z(nr[s], lr[s]) - TIME_STEP * up_r(nz[s])
                e_new[2, k] = ez[s] + (up_r(inner * nf[s]) - signed[s] * nr[t]) * per_outer
            return carry
        lax.fori_loop(0, OWN // 2, pair, 0)

    for copy in halo1:
        copy.wait_recv()
    maxwell(e0, h0, below1, above1, h1, x1)
    go2[0]()

    for copy in loads[2:]:
        copy.wait()
    stiff, damp, couple, harden = (mat[i : i + 1, :] for i in range(4))
    over = 1.0 / (1.0 + 0.5 * damp)
    packed = jnp.concatenate(
        [(1.0 - 0.5 * damp) * over, stiff * couple * over, stiff * over, 0.1 * harden * over]
        + [jnp.zeros((124, R), F32)],
        axis=0,
    )
    for half in range(2):
        turned = packed[:, half * 128 : half * 128 + 128].T
        for i in range(4):
            coef[i, pl.ds(half * 128, 128), :] = jnp.broadcast_to(turned[:, i : i + 1], (128, 128))

    weight = jnp.where(
        lax.broadcasted_iota(jnp.int32, (M, 1), 0) == 0, 1.0 / NA, 2.0 / NA
    ).astype(F32)

    def gas(field, sub, change):
        def forward(c, carry):
            value = field[c] if sub is None else field[c] - sub[c]
            pts[c] = dot3(split(value.T), (tab[0], tab[1]), ((1,), (0,)))
            return carry
        lax.fori_loop(0, 3, forward, 0)

        def block(b, carry):
            at = pl.ds(pl.multiple_of(b * 8, 8), 8)
            keep, drive, pull, soft = (coef[i, at, :] for i in range(4))
            for q in range(NA // 128):
                n = pl.ds(q * 128, 128)
                p = [pol[c, at, n] for c in range(3)]
                v = [vel[c, at, n] for c in range(3)]
                u = [drive * pts[c, at, n] for c in range(3)]
                start = list(p)
                for _ in range(SUBSTEPS):
                    energy = p[0] * p[0] + p[1] * p[1] + p[2] * p[2]
                    rate = pull + soft * energy
                    for c in range(3):
                        v[c] = keep * v[c] + u[c] - rate * p[c]
                        p[c] = p[c] + v[c]
                for c in range(3):
                    pol[c, at, n] = p[c]
                    vel[c, at, n] = v[c]
                    pts[c, at, n] = p[c] - start[c]
            return carry
        lax.fori_loop(0, R // 8, block, 0)

        def backward(c, carry):
            change[c] = weight * dot3((tab[0], tab[1]), split(pts[c]), ((1,), (1,)))
            return carry
        lax.fori_loop(0, 3, backward, 0)

    go1[1]()
    gas(f1, None, ch1)
    back1[0]()

    go2[1]()
    gas(f2, ch1, ch2)
    back2[0]()
    outs = [pltpu.make_async_copy(pol, p_out, out_sem.at[0]), pltpu.make_async_copy(vel, v_out, out_sem.at[1])]
    for copy in outs:
        copy.start()

    back1[1]()

    def subtract(a, b, out):
        def one(i, carry):
            for c in range(3):
                out[c, i] = a[c, i] - b[c, i]
            return carry
        lax.fori_loop(0, OWN, one, 0)

    subtract(x1, c1, e1)
    for copy in halo2:
        copy.start()
    for copy in halo2:
        copy.wait_recv()
    maxwell(e1, h1, below2, above2, h2, x2)
    outs.append(pltpu.make_async_copy(h2, h_out, out_sem.at[2]))
    outs[2].start()

    back2[1]()
    subtract(x2, c2, x2)
    outs.append(pltpu.make_async_copy(x2, e_out, out_sem.at[3]))
    outs[3].start()
    for stage in (go1, go2, back1, back2):
        stage[2]()
    for copy in halo1 + halo2:
        copy.wait_send()
    for copy in outs:
        copy.wait()


def on_device(efield, hfield, polar, velocity, material):
    field = pltpu.VMEM((3, OWN, OWN, R), F32)
    state = pltpu.VMEM((3, R, NA), F32)
    modes = pltpu.VMEM((3, M, R), F32)
    dma = pltpu.SemaphoreType.DMA
    anywhere = pl.BlockSpec(memory_space=pl.ANY)
    new_e, new_h, new_p, new_v = pl.pallas_call(
        kernel,
        out_shape=[
            jax.ShapeDtypeStruct((3, OWN, OWN, R), F32),
            jax.ShapeDtypeStruct((3, OWN, OWN, R), F32),
            jax.ShapeDtypeStruct((3, R, NA), F32),
            jax.ShapeDtypeStruct((3, R, NA), F32),
        ],
        in_specs=[anywhere] * 6,
        out_specs=[anywhere] * 4,
        scratch_shapes=[field] * 9 + [modes] * 4
        + [state] * 3
        + [
            pltpu.VMEM((4, R), F32),
            pltpu.VMEM((4, R, 128), F32),
            pltpu.VMEM((2, M, NA), BF16),
            pltpu.VMEM((5, OWN, R), F32),
            pltpu.VMEM((2, OWN, R), F32),
            pltpu.VMEM((5, OWN, R), F32),
            pltpu.VMEM((2, OWN, R), F32),
            dma((6,)), dma((4, OWN)), dma((4, OWN)), dma((4,)), dma((2, 3)), dma((2, 3)), dma((4,)),
        ],
        compiler_params=pltpu.CompilerParams(
            collective_id=0, has_side_effects=True, vmem_limit_bytes=40 << 20
        ),
        name="yee_gas",
    )(
        efield,
        hfield,
        polar.reshape(3, R, NA),
        velocity.reshape(3, R, NA),
        material.reshape(4, R),
        jnp.asarray(tables()),
    )
    shape = (3, 1, 1, R, NA)
    return new_e, new_h, new_p.reshape(shape), new_v.reshape(shape)


def solution(mesh):
    field, state = P(None, "mode", "gz", None), P(None, "gz", "mode", None, None)
    return jax.shard_map(
        on_device,
        mesh=mesh,
        in_specs=(field, field, state, state, P(None, "gz", "mode", None)),
        out_specs=(field, field, state, state),
        check_vma=False,
    )
```

profile of v0, /device:TPU:7, one launch (start us, length us, event | category | flops | bytes accessed | tf_op | source)
XLA Modules:
  0.0 102.0 jit_solution(9156046739442372224)
XLA Ops:
  0.6 0.7 copy.14
  1.3 0.0 copy-start
  1.3 1.4 %copy-done = f32[3,1,1,256,512]{4,3,2,1,0:T(8,128)S(1)} copy-done((f32[3,1,1,256,512]{4,3,2,1,0:T(8,128)S(1)}, f32[3,1,1,256,512]{4,3,2,1,0:T(8,128)}, u32[]{:S(2)}) %copy-start) | copy-done | bytes 1572888
  2.7 0.0 copy-start.1
  2.7 1.4 %copy-done.1 = f32[3,1,1,256,512]{4,3,2,1,0:T(8,128)S(1)} copy-done((f32[3,1,1,256,512]{4,3,2,1,0:T(8,128)S(1)}, f32[3,1,1,256,512]{4,3,2,1,0:T(8,128)}, u32[]{:S(2)}) %copy-start.1) | copy-done | bytes 1572888
  4.1 0.0 copy-start.2
  4.1 1.1 %copy-done.2 = f32[3,16,16,256]{3,2,1,0:T(8,128)S(1)} copy-done((f32[3,16,16,256]{3,2,1,0:T(8,128)S(1)}, f32[3,16,16,256]{3,2,1,0:T(8,128)}, u32[]{:S(2)}) %copy-start.2) | copy-done | bytes 786456
  5.3 0.0 copy-start.3
  5.3 1.1 %copy-done.3 = f32[3,16,16,256]{3,2,1,0:T(8,128)S(1)} copy-done((f32[3,16,16,256]{3,2,1,0:T(8,128)S(1)}, f32[3,16,16,256]{3,2,1,0:T(8,128)}, u32[]{:S(2)}) %copy-start.3) | copy-done | bytes 786456
  6.4 0.0 copy-start.4
  6.4 1.0 %copy-done.4 = bf16[2,256,512]{2,1,0:T(8,128)(2,1)S(1)} copy-done((bf16[2,256,512]{2,1,0:T(8,128)(2,1)S(1)}, bf16[2,256,512]{2,1,0:T(8,128)(2,1)}, u32[]{:S(2)}) %copy-start.4) | copy-done | bytes 524312
  7.4 90.5 %yee_gas.1 = (f32[3,16,16,256]{3,2,1,0:T(8,128)S(1)}, f32[3,16,16,256]{3,2,1,0:T(8,128)S(1)}, f32[3,256,512]{2,1,0:T(8,128)S(1)}, f32[3,256,512]{2,1,0:T(8,128)S(1)}) custom-call(f32[3,16,16,256]{3,2,1,0:T(8,128)S(1)} %copy-done.2, f32[3,16,16,256]{3,2,1,0:T(8,128)S(1)} %copy-done.3, f32[3,256,512]{2,1,0:T(8,128)S(1)} %bitcast.13, ...), custom_call_target="tpu_custom_call" | custom-call | tf_op jit(solution)/shard_map/yee_gas/pallas_call | solution.py:276
  98.0 0.9 copy.19
  98.9 0.9 copy.20
  99.7 1.1 %copy.21 = f32[3,1,1,256,512]{4,3,2,1,0:T(8,128)} copy(f32[3,1,1,256,512]{4,3,2,1,0:T(8,128)S(1)} %bitcast.12) | data formatting | bytes 3145728
  100.9 1.1 %copy.22 = f32[3,1,1,256,512]{4,3,2,1,0:T(8,128)} copy(f32[3,1,1,256,512]{4,3,2,1,0:T(8,128)S(1)} %bitcast.11) | data formatting | bytes 3145728
Async XLA Ops:
  1.3 1.4 %copy-start = (f32[3,1,1,256,512]{4,3,2,1,0:T(8,128)S(1)}, f32[3,1,1,256,512]{4,3,2,1,0:T(8,128)}, u32[]{:S(2)}) copy-start(f32[3,1,1,256,512]{4,3,2,1,0:T(8,128)} %param.8) | copy-start | bytes 4718596
  2.7 1.4 %copy-start.1 = (f32[3,1,1,256,512]{4,3,2,1,0:T(8,128)S(1)}, f32[3,1,1,256,512]{4,3,2,1,0:T(8,128)}, u32[]{:S(2)}) copy-start(f32[3,1,1,256,512]{4,3,2,1,0:T(8,128)} %param.9) | copy-start | bytes 4718596
  4.1 1.1 %copy-start.2 = (f32[3,16,16,256]{3,2,1,0:T(8,128)S(1)}, f32[3,16,16,256]{3,2,1,0:T(8,128)}, u32[]{:S(2)}) copy-start(f32[3,16,16,256]{3,2,1,0:T(8,128)} %e_in.1) | copy-start | bytes 2359300
  5.3 1.1 %copy-start.3 = (f32[3,16,16,256]{3,2,1,0:T(8,128)S(1)}, f32[3,16,16,256]{3,2,1,0:T(8,128)}, u32[]{:S(2)}) copy-start(f32[3,16,16,256]{3,2,1,0:T(8,128)} %h_in.1) | copy-start | bytes 2359300
  6.4 1.0 %copy-start.4 = (bf16[2,256,512]{2,1,0:T(8,128)(2,1)S(1)}, bf16[2,256,512]{2,1,0:T(8,128)(2,1)}, u32[]{:S(2)}) copy-start(bf16[2,256,512]{2,1,0:T(8,128)(2,1)} %constant.2.clone.tab_in) | copy-start | bytes 1572868
where the time goes:
time: 102 us
  Pallas kernels  90.5 us (89%)
  local copies, waits for them, and re-layouts  10.9 us (11%)
    pallas_call x1, Pallas kernels, on_device(): pl.pallas_call(kernel, out_shape=[jax.ShapeDtypeStruct((3, OWN, OWN, R),...  90.5 us
    unnamed x15, local copies, waits for them, and re-layouts  10.9 us

commit v1 on v0

--- a/solution.py
+++ b/solution.py
@@ -46,10 +46,10 @@
 
 def kernel(
     e_in, h_in, p_in, v_in, mat_in, tab_in,
-    e_out, h_out, p_out, v_out,
-    e0, h0, h1, x1, e1, h2, x2, c1, c2, f1, f2, ch1, ch2,
-    pol, vel, pts, mat, coef, tab, below1, above1, below2, above2,
-    load_sem, send_sem, recv_sem, own_sem, halo_send, halo_recv, out_sem,
+    x2, h2, pol, vel,
+    e0, h0, h1, x1, e1, c1, c2, f1, f2, ch1, ch2,
+    pts, mat, coef, tab, below1, above1, below2, above2,
+    load_sem, send_sem, recv_sem, own_sem, halo_send, halo_recv,
 ):
     me = lax.axis_index("mode")
     gz = lax.axis_index("gz")
@@ -176,7 +176,7 @@
 
     for copy in loads[2:]:
         copy.wait()
-    stiff, damp, couple, harden = (mat[i : i + 1, :] for i in range(4))
+    stiff, damp, couple, harden = (mat[i, 0] for i in range(4))
     over = 1.0 / (1.0 + 0.5 * damp)
     packed = jnp.concatenate(
         [(1.0 - 0.5 * damp) * over, stiff * couple * over, stiff * over, 0.1 * harden * over]
@@ -233,9 +233,6 @@
     go2[1]()
     gas(f2, ch1, ch2)
     back2[0]()
-    outs = [pltpu.make_async_copy(pol, p_out, out_sem.at[0]), pltpu.make_async_copy(vel, v_out, out_sem.at[1])]
-    for copy in outs:
-        copy.start()
 
     back1[1]()
 
@@ -252,18 +249,23 @@
     for copy in halo2:
         copy.wait_recv()
     maxwell(e1, h1, below2, above2, h2, x2)
-    outs.append(pltpu.make_async_copy(h2, h_out, out_sem.at[2]))
-    outs[2].start()
 
     back2[1]()
     subtract(x2, c2, x2)
-    outs.append(pltpu.make_async_copy(x2, e_out, out_sem.at[3]))
-    outs[3].start()
     for stage in (go1, go2, back1, back2):
         stage[2]()
     for copy in halo1 + halo2:
         copy.wait_send()
-    for copy in outs:
+
+
+def finish(*refs):
+    half, sem = len(refs) // 2, refs[-1]
+    copies = [
+        pltpu.make_async_copy(refs[i], refs[half + i], sem.at[i]) for i in range(half)
+    ]
+    for copy in copies:
+        copy.start()
+    for copy in copies:
         copy.wait()
 
 
@@ -273,30 +275,31 @@
     modes = pltpu.VMEM((3, M, R), F32)
     dma = pltpu.SemaphoreType.DMA
     anywhere = pl.BlockSpec(memory_space=pl.ANY)
-    new_e, new_h, new_p, new_v = pl.pallas_call(
+    results = [
+        jax.ShapeDtypeStruct((3, OWN, OWN, R), F32),
+        jax.ShapeDtypeStruct((3, OWN, OWN, R), F32),
+        jax.ShapeDtypeStruct((3, R, NA), F32),
+        jax.ShapeDtypeStruct((3, R, NA), F32),
+    ]
+    made = pl.pallas_call(
         kernel,
-        out_shape=[
-            jax.ShapeDtypeStruct((3, OWN, OWN, R), F32),
-            jax.ShapeDtypeStruct((3, OWN, OWN, R), F32),
-            jax.ShapeDtypeStruct((3, R, NA), F32),
-            jax.ShapeDtypeStruct((3, R, NA), F32),
-        ],
+        out_shape=[pltpu.VMEM(r.shape, r.dtype) for r in results],
         in_specs=[anywhere] * 6,
-        out_specs=[anywhere] * 4,
-        scratch_shapes=[field] * 9 + [modes] * 4
-        + [state] * 3
+        out_specs=[pl.BlockSpec(memory_space=pltpu.VMEM)] * 4,
+        scratch_shapes=[field] * 7 + [modes] * 4
+        + [state]
         + [
-            pltpu.VMEM((4, R), F32),
+            pltpu.VMEM((4, 1, 1, R), F32),
             pltpu.VMEM((4, R, 128), F32),
             pltpu.VMEM((2, M, NA), BF16),
             pltpu.VMEM((5, OWN, R), F32),
             pltpu.VMEM((2, OWN, R), F32),
             pltpu.VMEM((5, OWN, R), F32),
             pltpu.VMEM((2, OWN, R), F32),
-            dma((6,)), dma((4, OWN)), dma((4, OWN)), dma((4,)), dma((2, 3)), dma((2, 3)), dma((4,)),
+            dma((6,)), dma((4, OWN)), dma((4, OWN)), dma((4,)), dma((2, 3)), dma((2, 3)),
         ],
         compiler_params=pltpu.CompilerParams(
-            collective_id=0, has_side_effects=True, vmem_limit_bytes=40 << 20
+            collective_id=0, has_side_effects=True, vmem_limit_bytes=59 << 20
         ),
         name="yee_gas",
     )(
@@ -304,9 +307,18 @@
         hfield,
         polar.reshape(3, R, NA),
         velocity.reshape(3, R, NA),
-        material.reshape(4, R),
+        material,
         jnp.asarray(tables()),
     )
+    new_e, new_h, new_p, new_v = pl.pallas_call(
+        finish,
+        out_shape=results,
+        in_specs=[pl.BlockSpec(memory_space=pltpu.VMEM)] * 4,
+        out_specs=[anywhere] * 4,
+        scratch_shapes=[dma((4,))],
+        compiler_params=pltpu.CompilerParams(vmem_limit_bytes=8 << 20),
+        name="finish",
+    )(*made)
     shape = (3, 1, 1, R, NA)
     return new_e, new_h, new_p.reshape(shape), new_v.reshape(shape)
 

time: 102 us -> 93.5 us (0.917)
  local copies, waits for them, and re-layouts: 10.9 us -> 0 us
  Pallas kernels: 90.5 us -> 92.7 us
    unnamed x15 -> x0, local copies, waits for them, and re-layouts: 10.9 us -> none
    pallas_call x1 -> x2, Pallas kernels: 90.5 us -> 92.7 us  [the longest x1 90.5 us: on_device(): pl.pallas_call(kernel, out_shape=[pltpu.VMEM(r.shape, r.dtype) for r in r...]
where the time goes in v1:
time: 93.5 us; the launch traced here: 93.3 us
  Pallas kernels  92.7 us (99%)
    pallas_call x1, Pallas kernels, on_device(): pl.pallas_call(kernel, out_shape=[pltpu.VMEM(r.shape, r.dtype) for r in r...  90.5 us
    pallas_call x1, Pallas kernels, on_device(): pl.pallas_call(finish, out_shape=results, in_specs=[pl.BlockSpec(memory_s...  2.22 us

profile of v1, /device:TPU:7, one launch (start us, length us, event | category | flops | bytes accessed | tf_op | source)
XLA Modules:
  0.0 93.3 jit_solution(10681448580137778449)
XLA Ops:
  0.6 90.5 %yee_gas.1 = (f32[3,16,16,256]{3,2,1,0:T(8,128)S(1)}, f32[3,16,16,256]{3,2,1,0:T(8,128)S(1)}, f32[3,256,512]{2,1,0:T(8,128)S(1)}, f32[3,256,512]{2,1,0:T(8,128)S(1)}) custom-call(f32[3,16,16,256]{3,2,1,0:T(8,128)} %e_in.1, f32[3,16,16,256]{3,2,1,0:T(8,128)} %h_in.1, f32[3,256,512]{2,1,0:T(8,128)} %bitcast.8, f32[3,256,512]{2,1,0:T(8,128)} %bitcast.9, ...), custom_call_target="tpu_custom_call" | custom-call | tf_op jit(solution)/shard_map/yee_gas/pallas_call | solution.py:284
  91.1 2.2 %finish.1 = (f32[3,16,16,256]{3,2,1,0:T(8,128)}, f32[3,16,16,256]{3,2,1,0:T(8,128)}, f32[3,256,512]{2,1,0:T(8,128)}, f32[3,256,512]{2,1,0:T(8,128)}) custom-call(f32[3,16,16,256]{3,2,1,0:T(8,128)S(1)} %get-tuple-element.12.refs_0_, f32[3,16,16,256]{3,2,1,0:T(8,128)S(1)} %get-tuple-element.13.refs_1_, f32[3,256,512]{2,1,0:T(8,128)S(1)} %get-tuple-element.14.refs_2_, ...), custom_call_target="tpu_custom_call" | custom-call | tf_op jit(solution)/shard_map/finish/pallas_call | solution.py:313

commit v2 on v1

--- a/solution.py
+++ b/solution.py
@@ -47,9 +47,9 @@
 def kernel(
     e_in, h_in, p_in, v_in, mat_in, tab_in,
     x2, h2, pol, vel,
-    e0, h0, h1, x1, e1, c1, c2, f1, f2, ch1, ch2,
-    pts, mat, coef, tab, below1, above1, below2, above2,
-    load_sem, send_sem, recv_sem, own_sem, halo_send, halo_recv,
+    e0, h0, h1, x1, e1, c1, c2, curl1, f1, f2, ch1, ch2,
+    pts, mat, coef, tab, below1, above1, below2, above2, before,
+    load_sem, send_sem, recv_sem, own_sem, halo_send, halo_recv, next_sem,
 ):
     me = lax.axis_index("mode")
     gz = lax.axis_index("gz")
@@ -57,11 +57,16 @@
     up, down = lax.rem(gz + 1, G), lax.rem(gz + G - 1, G)
 
     def each(fn):
-        for dz in range(4):
-            def body(dy, carry, dz=dz):
-                fn(dz * 4 + dy, lax.rem(zh + dz, 4) * 4 + lax.rem(y + dy, 4))
-                return carry
-            lax.fori_loop(1 if dz == 0 else 0, 4, body, 0)
+        def body(dy, carry):
+            for dz in (2, 1, 3, 0):
+                def one(dz=dz):
+                    fn(dz * 4 + dy, lax.rem(zh + dz, 4) * 4 + lax.rem(y + dy, 4))
+                if dz == 0:
+                    pl.when(dy > 0)(one)
+                else:
+                    one()
+            return carry
+        lax.fori_loop(0, 4, body, 0)
 
     loads = [
         pltpu.make_async_copy(s, d, load_sem.at[i])
@@ -102,9 +107,42 @@
     mine = pl.ds(pl.multiple_of(me * OWN, OWN), OWN)
     rows = lambda p: pl.ds(pl.multiple_of(p * OWN, OWN), OWN)
     go1 = exchange(0, lambda p: e_in.at[:, :, p, :], f1.at[:, mine, :])
-    go2 = exchange(1, lambda p: x1.at[:, :, p, :], f2.at[:, mine, :])
     back1 = exchange(2, lambda p: ch1.at[:, rows(p), :], c1.at[:, :, me, :])
     back2 = exchange(3, lambda p: ch2.at[:, rows(p), :], c2.at[:, :, me, :])
+
+    def part(stage, i, p, comps):
+        return pltpu.make_async_remote_copy(
+            curl1.at[comps, :, p, :], f2.at[comps, mine, :],
+            send_sem.at[stage, i], recv_sem.at[stage, i], device_id={"mode": p}, device_id_type=MESH,
+        )
+
+    AXIAL, RADIAL, REST = pl.ds(0, 1), pl.ds(1, 1), pl.ds(1, 2)
+
+    def rest(i, p, whole, act):
+        pl.when(whole)(lambda: act(part(4, i, p, REST)))
+        pl.when(jnp.logical_not(whole))(lambda: act(part(4, i, p, RADIAL)))
+
+    own2 = pltpu.make_async_copy(curl1.at[:, :, me, :], f2.at[:, mine, :], own_sem.at[1])
+    follow = pltpu.make_async_remote_copy(
+        f2.at[0], before, next_sem.at[0], next_sem.at[1],
+        device_id={"mode": jnp.minimum(me + 1, OWN - 1)}, device_id_type=MESH,
+    )
+
+    def go2_start():
+        own2.start()
+        each(lambda i, p: part(1, i, p, AXIAL).start())
+        each(lambda i, p: rest(i, p, lax.rem(p, 4) == 0, lambda c: c.start()))
+
+    def go2_wait_axial():
+        own2.wait()
+        each(lambda i, p: part(1, i, p, AXIAL).wait_recv())
+
+    def go2_wait_rest():
+        each(lambda i, p: rest(i, p, y == 0, lambda c: c.wait_recv()))
+
+    def go2_wait_send():
+        each(lambda i, p: part(1, i, p, AXIAL).wait_send())
+        each(lambda i, p: rest(i, p, lax.rem(p, 4) == 0, lambda c: c.wait_send()))
 
     def halo(stage, e, h, below, above):
         def make(i, source, target, to):
@@ -138,7 +176,7 @@
     up_z = lambda f, row: jnp.where(plane == OWN - 1, row, pltpu.roll(f, OWN - 1, 0)) - f
     down_z = lambda f, row: f - jnp.where(plane == 0, row, pltpu.roll(f, 1, 0))
 
-    def maxwell(e, h, below, above, h_new, e_new):
+    def maxwell(e, h, below, above, h_new, e_new, curl=None):
         def pair(a, carry):
             order = (me * (OWN // 2) + a).astype(F32)
             signed = (order, -order)
@@ -159,20 +197,31 @@
                 f = bhf[s] - RATIO * (er[s][0:1] - ber[s]) + TIME_STEP * down_r(bez[s])
                 lr.append(jnp.where(gz == 0, 0.0, r))
                 lf.append(jnp.where(gz == 0, 0.0, f))
+            made = []
             for s in range(2):
                 t = 1 - s
                 k = 2 * a + s
                 h_new[0, k], h_new[1, k], h_new[2, k] = nr[s], nf[s], nz[s]
-                e_new[0, k] = er[s] + (signed[s] * nz[t]) * per_inner - RATIO * down_z(nf[s], lf[s])
-                e_new[1, k] = ef[s] + RATIO * down_z(nr[s], lr[s]) - TIME_STEP * up_r(nz[s])
-                e_new[2, k] = ez[s] + (up_r(inner * nf[s]) - signed[s] * nr[t]) * per_outer
+                gr = (signed[s] * nz[t]) * per_inner - RATIO * down_z(nf[s], lf[s])
+                gf = RATIO * down_z(nr[s], lr[s]) - TIME_STEP * up_r(nz[s])
+                gz_ = (up_r(inner * nf[s]) - signed[s] * nr[t]) * per_outer
+                e_new[0, k], e_new[1, k], e_new[2, k] = er[s] + gr, ef[s] + gf, ez[s] + gz_
+                made.append((gz_, gr, gf))
+            if curl is not None:
+                for s in range(2):
+                    for c in range(3):
+                        curl[c, 2 * a + s] = made[s][c]
+
+                @pl.when(me * (OWN // 2) + a == 0)
+                def _():
+                    curl[0, 1] = made[0][2]
             return carry
         lax.fori_loop(0, OWN // 2, pair, 0)
 
     for copy in halo1:
         copy.wait_recv()
-    maxwell(e0, h0, below1, above1, h1, x1)
-    go2[0]()
+    maxwell(e0, h0, below1, above1, h1, x1, curl1)
+    go2_start()
 
     for copy in loads[2:]:
         copy.wait()
@@ -192,9 +241,24 @@
         lax.broadcasted_iota(jnp.int32, (M, 1), 0) == 0, 1.0 / NA, 2.0 / NA
     ).astype(F32)
 
-    def gas(field, sub, change):
+    def complete():
+        def block(b, carry):
+            at = pl.ds(pl.multiple_of(b * OWN, OWN), OWN)
+            axial, radial = f2[0, at, :], f2[1, at, :]
+            total = up_r(inner * radial) + (RATIO / TIME_STEP) * (outer * (axial - before[at, :]))
+            mode = lax.broadcasted_iota(jnp.int32, (OWN, 1), 0) + b * OWN
+            order = (mode // 2).astype(F32)
+            per_order = jnp.where(mode < 2, 0.0, 1.0 / jnp.maximum(order, 1.0))
+            turned = jnp.where(
+                lax.rem(mode, 2) == 0, pltpu.roll(total, OWN - 1, 0), -pltpu.roll(total, 1, 0)
+            )
+            f2[2, at, :] = jnp.where(mode == 0, pltpu.roll(axial, OWN - 1, 0), turned * per_order)
+            return carry
+        lax.fori_loop(0, M // OWN, block, 0)
+
+    def gas(field, add, sub, change):
         def forward(c, carry):
-            value = field[c] if sub is None else field[c] - sub[c]
+            value = field[c] if sub is None else field[c] + (add[lax.rem(c + 1, 3)] - sub[c])
             pts[c] = dot3(split(value.T), (tab[0], tab[1]), ((1,), (0,)))
             return carry
         lax.fori_loop(0, 3, forward, 0)
@@ -227,11 +291,18 @@
         lax.fori_loop(0, 3, backward, 0)
 
     go1[1]()
-    gas(f1, None, ch1)
+    gas(f1, None, None, ch1)
+    go2_wait_axial()
+    pl.when(y < 3)(lambda: follow.start())
+    go2_wait_rest()
     back1[0]()
 
-    go2[1]()
-    gas(f2, ch1, ch2)
+    @pl.when(y > 0)
+    def _():
+        follow.wait_recv()
+        complete()
+
+    gas(f1, f2, ch1, ch2)
     back2[0]()
 
     back1[1]()
@@ -252,8 +323,10 @@
 
     back2[1]()
     subtract(x2, c2, x2)
-    for stage in (go1, go2, back1, back2):
+    for stage in (go1, back1, back2):
         stage[2]()
+    go2_wait_send()
+    pl.when(y < 3)(lambda: follow.wait_send())
     for copy in halo1 + halo2:
         copy.wait_send()
 
@@ -286,7 +359,7 @@
         out_shape=[pltpu.VMEM(r.shape, r.dtype) for r in results],
         in_specs=[anywhere] * 6,
         out_specs=[pl.BlockSpec(memory_space=pltpu.VMEM)] * 4,
-        scratch_shapes=[field] * 7 + [modes] * 4
+        scratch_shapes=[field] * 8 + [modes] * 4
         + [state]
         + [
             pltpu.VMEM((4, 1, 1, R), F32),
@@ -296,7 +369,8 @@
             pltpu.VMEM((2, OWN, R), F32),
             pltpu.VMEM((5, OWN, R), F32),
             pltpu.VMEM((2, OWN, R), F32),
-            dma((6,)), dma((4, OWN)), dma((4, OWN)), dma((4,)), dma((2, 3)), dma((2, 3)),
+            pltpu.VMEM((M, R), F32),
+            dma((6,)), dma((5, OWN)), dma((5, OWN)), dma((4,)), dma((2, 3)), dma((2, 3)), dma((2,)),
         ],
         compiler_params=pltpu.CompilerParams(
             collective_id=0, has_side_effects=True, vmem_limit_bytes=59 << 20

time: 93.5 us -> 85.1 us (0.910); the launches traced: 93.3 us -> 83.9 us
  Pallas kernels: 92.7 us -> 83.3 us
    pallas_call x1, Pallas kernels: 90.5 us -> 81.1 us  [on_device(): pl.pallas_call(kernel, out_shape=[pltpu.VMEM(r.shape, r.dtype) for r in r...]
where the time goes in v2:
time: 85.1 us; the launch traced here: 83.9 us
  Pallas kernels  83.3 us (98%)
    pallas_call x1, Pallas kernels, on_device(): pl.pallas_call(kernel, out_shape=[pltpu.VMEM(r.shape, r.dtype) for r in r...  81.1 us
    pallas_call x1, Pallas kernels, on_device(): pl.pallas_call(finish, out_shape=results, in_specs=[pl.BlockSpec(memory_s...  2.22 us

profile of v2, /device:TPU:7, one launch (start us, length us, event | category | flops | bytes accessed | tf_op | source)
XLA Modules:
  0.0 83.9 jit_solution(15873671211970822917)
XLA Ops:
  0.6 81.1 %yee_gas.1 = (f32[3,16,16,256]{3,2,1,0:T(8,128)S(1)}, f32[3,16,16,256]{3,2,1,0:T(8,128)S(1)}, f32[3,256,512]{2,1,0:T(8,128)S(1)}, f32[3,256,512]{2,1,0:T(8,128)S(1)}) custom-call(f32[3,16,16,256]{3,2,1,0:T(8,128)} %e_in.1, f32[3,16,16,256]{3,2,1,0:T(8,128)} %h_in.1, f32[3,256,512]{2,1,0:T(8,128)} %bitcast.8, f32[3,256,512]{2,1,0:T(8,128)} %bitcast.9, ...), custom_call_target="tpu_custom_call" | custom-call | tf_op jit(solution)/shard_map/yee_gas/pallas_call | solution.py:357
  81.7 2.2 %finish.1 = (f32[3,16,16,256]{3,2,1,0:T(8,128)}, f32[3,16,16,256]{3,2,1,0:T(8,128)}, f32[3,256,512]{2,1,0:T(8,128)}, f32[3,256,512]{2,1,0:T(8,128)}) custom-call(f32[3,16,16,256]{3,2,1,0:T(8,128)S(1)} %get-tuple-element.12.refs_0_, f32[3,16,16,256]{3,2,1,0:T(8,128)S(1)} %get-tuple-element.13.refs_1_, f32[3,256,512]{2,1,0:T(8,128)S(1)} %get-tuple-element.14.refs_2_, ...), custom_call_target="tpu_custom_call" | custom-call | tf_op jit(solution)/shard_map/finish/pallas_call | solution.py:387

commit v3 on v2

--- a/solution.py
+++ b/solution.py
@@ -48,8 +48,8 @@
     e_in, h_in, p_in, v_in, mat_in, tab_in,
     x2, h2, pol, vel,
     e0, h0, h1, x1, e1, c1, c2, curl1, f1, f2, ch1, ch2,
-    pts, mat, coef, tab, below1, above1, below2, above2, before,
-    load_sem, send_sem, recv_sem, own_sem, halo_send, halo_recv, next_sem,
+    pts, mat, coef, tab, below1, above1, below2, above2, before, after, psi, gauge_r, gauge_z, relay,
+    load_sem, send_sem, recv_sem, own_sem, halo_send, halo_recv, next_sem, relay_send, relay_recv,
 ):
     me = lax.axis_index("mode")
     gz = lax.axis_index("gz")
@@ -77,6 +77,11 @@
     for copy in loads:
         copy.start()
 
+    def clear(i, carry):
+        c1[2, i] = jnp.zeros((OWN, R), F32)
+        return carry
+    lax.fori_loop(0, OWN, clear, 0)
+
     barrier = pltpu.get_barrier_semaphore()
     each(lambda i, p: pl.semaphore_signal(barrier, 1, device_id={"mode": p}, device_id_type=MESH))
     pl.semaphore_signal(barrier, 1, device_id={"gz": up}, device_id_type=MESH)
@@ -107,7 +112,8 @@
     mine = pl.ds(pl.multiple_of(me * OWN, OWN), OWN)
     rows = lambda p: pl.ds(pl.multiple_of(p * OWN, OWN), OWN)
     go1 = exchange(0, lambda p: e_in.at[:, :, p, :], f1.at[:, mine, :])
-    back1 = exchange(2, lambda p: ch1.at[:, rows(p), :], c1.at[:, :, me, :])
+    back_r = exchange(2, lambda p: gauge_r.at[rows(p), :], c1.at[1, :, me, :])
+    back_z = exchange(5, lambda p: gauge_z.at[rows(p), :], c1.at[0, :, me, :])
     back2 = exchange(3, lambda p: ch2.at[:, rows(p), :], c2.at[:, :, me, :])
 
     def part(stage, i, p, comps):
@@ -121,6 +127,46 @@
     def rest(i, p, whole, act):
         pl.when(whole)(lambda: act(part(4, i, p, REST)))
         pl.when(jnp.logical_not(whole))(lambda: act(part(4, i, p, RADIAL)))
+
+    def spread(line, to):
+        return pltpu.make_async_remote_copy(
+            ch1.at[1, rows(to * 4 + line), :], relay.at[to],
+            relay_send.at[line * 4 + to], relay_recv.at[to],
+            device_id={"mode": zh * 4 + line}, device_id_type=MESH,
+        )
+
+    def each_spread(act):
+        def body(i, carry):
+            act(spread(i // 4, lax.rem(i, 4)))
+            return carry
+        lax.fori_loop(4, 16, body, 0)
+
+    def relayed(act):
+        def body(to, carry):
+            act(spread(1, to))
+            return carry
+        lax.fori_loop(0, 4, body, 0)
+
+    def phi(dz, source):
+        to = lax.rem(zh + dz, 4)
+        source = ch1.at[1, rows(to * 4), :] if source is None else source.at[to]
+        target = c1.at[2, :, zh * 4, :]
+        if dz == 0:
+            return pltpu.make_async_copy(source, target, own_sem.at[6])
+        return pltpu.make_async_remote_copy(
+            source, target, send_sem.at[6, dz], recv_sem.at[6, dz],
+            device_id={"mode": to * 4 + y}, device_id_type=MESH,
+        )
+
+    def each_phi(act):
+        for dz in (2, 1, 3, 0):
+            pl.when(y == 0)(lambda: act(phi(dz, None), dz))
+            pl.when(y > 0)(lambda: act(phi(dz, relay), dz))
+
+    lead = pltpu.make_async_remote_copy(
+        psi, after, next_sem.at[2], next_sem.at[3],
+        device_id={"mode": jnp.maximum(me - 1, 0)}, device_id_type=MESH,
+    )
 
     own2 = pltpu.make_async_copy(curl1.at[:, :, me, :], f2.at[:, mine, :], own_sem.at[1])
     follow = pltpu.make_async_remote_copy(
@@ -176,7 +222,7 @@
     up_z = lambda f, row: jnp.where(plane == OWN - 1, row, pltpu.roll(f, OWN - 1, 0)) - f
     down_z = lambda f, row: f - jnp.where(plane == 0, row, pltpu.roll(f, 1, 0))
 
-    def maxwell(e, h, below, above, h_new, e_new, curl=None):
+    def maxwell(e, h, below, above, h_new, e_new, curl=None, base=None):
         def pair(a, carry):
             order = (me * (OWN // 2) + a).astype(F32)
             signed = (order, -order)
@@ -205,7 +251,11 @@
                 gr = (signed[s] * nz[t]) * per_inner - RATIO * down_z(nf[s], lf[s])
                 gf = RATIO * down_z(nr[s], lr[s]) - TIME_STEP * up_r(nz[s])
                 gz_ = (up_r(inner * nf[s]) - signed[s] * nr[t]) * per_outer
-                e_new[0, k], e_new[1, k], e_new[2, k] = er[s] + gr, ef[s] + gf, ez[s] + gz_
+                if base is None:
+                    e_new[0, k], e_new[1, k], e_new[2, k] = er[s] + gr, ef[s] + gf, ez[s] + gz_
+                else:
+                    for c, g in enumerate((gr, gf, gz_)):
+                        e_new[c, k] = base[c, k] + g
                 made.append((gz_, gr, gf))
             if curl is not None:
                 for s in range(2):
@@ -241,18 +291,43 @@
         lax.broadcasted_iota(jnp.int32, (M, 1), 0) == 0, 1.0 / NA, 2.0 / NA
     ).astype(F32)
 
+    def unrotate(value, b):
+        mode = lax.broadcasted_iota(jnp.int32, (OWN, 1), 0) + b * OWN
+        per_order = jnp.where(mode < 2, 0.0, 1.0 / jnp.maximum((mode // 2).astype(F32), 1.0))
+        turned = jnp.where(
+            lax.rem(mode, 2) == 0, -pltpu.roll(value, OWN - 1, 0), pltpu.roll(value, 1, 0)
+        )
+        return mode, turned * per_order
+
+    def block_rows(b):
+        return pl.ds(pl.multiple_of(b * OWN, OWN), OWN)
+
+    def gauge_radial():
+        def block(b, carry):
+            at = block_rows(b)
+            value = jnp.where(y > 0, outer * ch1[1, at, :], 0.0)
+            psi[at, :] = value
+            gauge_r[at, :] = ch1[0, at, :] - unrotate(down_r(value), b)[1]
+            return carry
+        lax.fori_loop(0, M // OWN, block, 0)
+
+    def gauge_axial():
+        def block(b, carry):
+            at = block_rows(b)
+            step = jnp.where(y < 3, after[at, :], 0.0) - psi[at, :]
+            mode, made = unrotate(step, b)
+            value = ch1[2, at, :] - (RATIO / TIME_STEP) * made
+            gauge_z[at, :] = jnp.where(mode == 1, pltpu.roll(ch1[1, at, :], 1, 0), value)
+            return carry
+        lax.fori_loop(0, M // OWN, block, 0)
+
     def complete():
         def block(b, carry):
             at = pl.ds(pl.multiple_of(b * OWN, OWN), OWN)
             axial, radial = f2[0, at, :], f2[1, at, :]
             total = up_r(inner * radial) + (RATIO / TIME_STEP) * (outer * (axial - before[at, :]))
-            mode = lax.broadcasted_iota(jnp.int32, (OWN, 1), 0) + b * OWN
-            order = (mode // 2).astype(F32)
-            per_order = jnp.where(mode < 2, 0.0, 1.0 / jnp.maximum(order, 1.0))
-            turned = jnp.where(
-                lax.rem(mode, 2) == 0, pltpu.roll(total, OWN - 1, 0), -pltpu.roll(total, 1, 0)
-            )
-            f2[2, at, :] = jnp.where(mode == 0, pltpu.roll(axial, OWN - 1, 0), turned * per_order)
+            mode, made = unrotate(-total, b)
+            f2[2, at, :] = jnp.where(mode == 0, pltpu.roll(axial, OWN - 1, 0), made)
             return carry
         lax.fori_loop(0, M // OWN, block, 0)
 
@@ -286,16 +361,25 @@
         lax.fori_loop(0, R // 8, block, 0)
 
         def backward(c, carry):
-            change[c] = weight * dot3((tab[0], tab[1]), split(pts[c]), ((1,), (1,)))
+            made = weight * dot3((tab[0], tab[1]), split(pts[c]), ((1,), (1,)))
+            change[c] = made if sub is None else sub[c] + made
             return carry
         lax.fori_loop(0, 3, backward, 0)
 
     go1[1]()
     gas(f1, None, None, ch1)
+    gauge_radial()
+    pl.when(y > 0)(lambda: lead.start())
+    pl.when(y == 0)(lambda: each_spread(lambda c: c.start()))
     go2_wait_axial()
     pl.when(y < 3)(lambda: follow.start())
     go2_wait_rest()
-    back1[0]()
+    back_r[0]()
+    pl.when(y < 3)(lambda: lead.wait_recv())
+    gauge_axial()
+    back_z[0]()
+    pl.when(y > 0)(lambda: relayed(lambda c: c.wait_recv()))
+    each_phi(lambda c, dz: c.start())
 
     @pl.when(y > 0)
     def _():
@@ -305,28 +389,41 @@
     gas(f1, f2, ch1, ch2)
     back2[0]()
 
-    back1[1]()
-
-    def subtract(a, b, out):
-        def one(i, carry):
-            for c in range(3):
-                out[c, i] = a[c, i] - b[c, i]
-            return carry
-        lax.fori_loop(0, OWN, one, 0)
-
-    subtract(x1, c1, e1)
+    back_r[1]()
+    back_z[1]()
+    each_phi(lambda c, dz: c.wait_recv() if dz else c.wait())
+
+    def subtract(i, carry):
+        for c in range(3):
+            e1[c, i] = x1[c, i] - c1[(c + 1) % 3, i]
+        return carry
+    lax.fori_loop(0, OWN, subtract, 0)
+
+    @pl.when(me == 0)
+    def _():
+        e1[1, 0] = x1[1, 0] - c1[0, 1]
+        e1[2, 1] = x1[2, 1]
+
     for copy in halo2:
         copy.start()
     for copy in halo2:
         copy.wait_recv()
-    maxwell(e1, h1, below2, above2, h2, x2)
+    maxwell(e1, h1, below2, above2, h2, x2, base=x1)
 
     back2[1]()
-    subtract(x2, c2, x2)
-    for stage in (go1, back1, back2):
+
+    def finish_e(i, carry):
+        for c in range(3):
+            x2[c, i] = x2[c, i] - c2[c, i]
+        return carry
+    lax.fori_loop(0, OWN, finish_e, 0)
+    for stage in (go1, back_r, back_z, back2):
         stage[2]()
     go2_wait_send()
     pl.when(y < 3)(lambda: follow.wait_send())
+    pl.when(y > 0)(lambda: lead.wait_send())
+    pl.when(y == 0)(lambda: each_spread(lambda c: c.wait_send()))
+    each_phi(lambda c, dz: c.wait_send() if dz else None)
     for copy in halo1 + halo2:
         copy.wait_send()
 
@@ -370,7 +467,13 @@
             pltpu.VMEM((5, OWN, R), F32),
             pltpu.VMEM((2, OWN, R), F32),
             pltpu.VMEM((M, R), F32),
-            dma((6,)), dma((5, OWN)), dma((5, OWN)), dma((4,)), dma((2, 3)), dma((2, 3)), dma((2,)),
+            pltpu.VMEM((M, R), F32),
+            pltpu.VMEM((M, R), F32),
+            pltpu.VMEM((M, R), F32),
+            pltpu.VMEM((M, R), F32),
+            pltpu.VMEM((4, OWN, R), F32),
+            dma((6,)), dma((7, OWN)), dma((7, OWN)), dma((7,)), dma((2, 3)), dma((2, 3)), dma((4,)),
+            dma((OWN,)), dma((4,)),
         ],
         compiler_params=pltpu.CompilerParams(
             collective_id=0, has_side_effects=True, vmem_limit_bytes=59 << 20

time: 85.1 us -> 84.8 us (level); the launches traced: 83.9 us -> 84.7 us
  no operation moved by 1% of the time
where the time goes in v3:
time: 84.8 us; the launch traced here: 84.7 us
  Pallas kernels  84.1 us (99%)
    pallas_call x1, Pallas kernels, on_device(): pl.pallas_call(kernel, out_shape=[pltpu.VMEM(r.shape, r.dtype) for r in r...  81.8 us
    pallas_call x1, Pallas kernels, on_device(): pl.pallas_call(finish, out_shape=results, in_specs=[pl.BlockSpec(memory_s...  2.22 us

profile of v3, /device:TPU:7, one launch (start us, length us, event | category | flops | bytes accessed | tf_op | source)
XLA Modules:
  0.0 84.7 jit_solution(11403725544028727386)
XLA Ops:
  0.6 81.8 %yee_gas.1 = (f32[3,16,16,256]{3,2,1,0:T(8,128)S(1)}, f32[3,16,16,256]{3,2,1,0:T(8,128)S(1)}, f32[3,256,512]{2,1,0:T(8,128)S(1)}, f32[3,256,512]{2,1,0:T(8,128)S(1)}) custom-call(f32[3,16,16,256]{3,2,1,0:T(8,128)} %e_in.1, f32[3,16,16,256]{3,2,1,0:T(8,128)} %h_in.1, f32[3,256,512]{2,1,0:T(8,128)} %bitcast.8, f32[3,256,512]{2,1,0:T(8,128)} %bitcast.9, ...), custom_call_target="tpu_custom_call" | custom-call | tf_op jit(solution)/shard_map/yee_gas/pallas_call | solution.py:454
  82.5 2.2 %finish.1 = (f32[3,16,16,256]{3,2,1,0:T(8,128)}, f32[3,16,16,256]{3,2,1,0:T(8,128)}, f32[3,256,512]{2,1,0:T(8,128)}, f32[3,256,512]{2,1,0:T(8,128)}) custom-call(f32[3,16,16,256]{3,2,1,0:T(8,128)S(1)} %get-tuple-element.12.refs_0_, f32[3,16,16,256]{3,2,1,0:T(8,128)S(1)} %get-tuple-element.13.refs_1_, f32[3,256,512]{2,1,0:T(8,128)S(1)} %get-tuple-element.14.refs_2_, ...), custom_call_target="tpu_custom_call" | custom-call | tf_op jit(solution)/shard_map/finish/pallas_call | solution.py:490

commit v4 on v3

--- a/solution.py
+++ b/solution.py
@@ -302,14 +302,20 @@
     def block_rows(b):
         return pl.ds(pl.multiple_of(b * OWN, OWN), OWN)
 
+    def gauge_psi():
+        def block(b, carry):
+            at = block_rows(b)
+            psi[at, :] = jnp.where(y > 0, outer * ch1[1, at, :], 0.0)
+            return carry
+        lax.fori_loop(0, M // OWN, block, 0, unroll=4)
+
     def gauge_radial():
         def block(b, carry):
             at = block_rows(b)
-            value = jnp.where(y > 0, outer * ch1[1, at, :], 0.0)
-            psi[at, :] = value
+            value = psi[at, :]
             gauge_r[at, :] = ch1[0, at, :] - unrotate(down_r(value), b)[1]
             return carry
-        lax.fori_loop(0, M // OWN, block, 0)
+        lax.fori_loop(0, M // OWN, block, 0, unroll=4)
 
     def gauge_axial():
         def block(b, carry):
@@ -319,7 +325,7 @@
             value = ch1[2, at, :] - (RATIO / TIME_STEP) * made
             gauge_z[at, :] = jnp.where(mode == 1, pltpu.roll(ch1[1, at, :], 1, 0), value)
             return carry
-        lax.fori_loop(0, M // OWN, block, 0)
+        lax.fori_loop(0, M // OWN, block, 0, unroll=4)
 
     def complete():
         def block(b, carry):
@@ -329,15 +335,16 @@
             mode, made = unrotate(-total, b)
             f2[2, at, :] = jnp.where(mode == 0, pltpu.roll(axial, OWN - 1, 0), made)
             return carry
-        lax.fori_loop(0, M // OWN, block, 0)
-
-    def gas(field, add, sub, change):
+        lax.fori_loop(0, M // OWN, block, 0, unroll=4)
+
+    def to_points(field, add, sub, first, last):
         def forward(c, carry):
             value = field[c] if sub is None else field[c] + (add[lax.rem(c + 1, 3)] - sub[c])
             pts[c] = dot3(split(value.T), (tab[0], tab[1]), ((1,), (0,)))
             return carry
-        lax.fori_loop(0, 3, forward, 0)
-
+        lax.fori_loop(first, last, forward, 0)
+
+    def respond():
         def block(b, carry):
             at = pl.ds(pl.multiple_of(b * 8, 8), 8)
             keep, drive, pull, soft = (coef[i, at, :] for i in range(4))
@@ -358,19 +365,25 @@
                     vel[c, at, n] = v[c]
                     pts[c, at, n] = p[c] - start[c]
             return carry
-        lax.fori_loop(0, R // 8, block, 0)
-
+        lax.fori_loop(0, R // 8, block, 0, unroll=2)
+
+    def to_modes(sub, change, first, last):
         def backward(c, carry):
             made = weight * dot3((tab[0], tab[1]), split(pts[c]), ((1,), (1,)))
             change[c] = made if sub is None else sub[c] + made
             return carry
-        lax.fori_loop(0, 3, backward, 0)
+        lax.fori_loop(first, last, backward, 0)
 
     go1[1]()
-    gas(f1, None, None, ch1)
-    gauge_radial()
+    to_points(f1, None, None, 0, 3)
+    respond()
+    to_modes(None, ch1, 1, 2)
+    gauge_psi()
     pl.when(y > 0)(lambda: lead.start())
     pl.when(y == 0)(lambda: each_spread(lambda c: c.start()))
+    to_modes(None, ch1, 0, 1)
+    to_modes(None, ch1, 2, 3)
+    gauge_radial()
     go2_wait_axial()
     pl.when(y < 3)(lambda: follow.start())
     go2_wait_rest()
@@ -380,15 +393,18 @@
     back_z[0]()
     pl.when(y > 0)(lambda: relayed(lambda c: c.wait_recv()))
     each_phi(lambda c, dz: c.start())
+    to_points(f1, f2, ch1, 0, 1)
+    to_points(f1, f2, ch1, 2, 3)
 
     @pl.when(y > 0)
     def _():
         follow.wait_recv()
         complete()
 
-    gas(f1, f2, ch1, ch2)
+    to_points(f1, f2, ch1, 1, 2)
+    respond()
+    to_modes(ch1, ch2, 0, 3)
     back2[0]()
-
     back_r[1]()
     back_z[1]()
     each_phi(lambda c, dz: c.wait_recv() if dz else c.wait())

time: 84.8 us -> 82.4 us (0.972)
  Pallas kernels: 84.1 us -> 81.7 us
    pallas_call x1, Pallas kernels: 81.8 us -> 79.4 us  [on_device(): pl.pallas_call(kernel, out_shape=[pltpu.VMEM(r.shape, r.dtype) for r in r...]
where the time goes in v4:
time: 82.4 us; the launch traced here: 82.3 us
  Pallas kernels  81.7 us (99%)
    pallas_call x1, Pallas kernels, on_device(): pl.pallas_call(kernel, out_shape=[pltpu.VMEM(r.shape, r.dtype) for r in r...  79.4 us
    pallas_call x1, Pallas kernels, on_device(): pl.pallas_call(finish, out_shape=results, in_specs=[pl.BlockSpec(memory_s...  2.22 us

profile of v4, /device:TPU:7, one launch (start us, length us, event | category | flops | bytes accessed | tf_op | source)
XLA Modules:
  0.0 82.3 jit_solution(15367004931349840135)
XLA Ops:
  0.6 79.4 %yee_gas.1 = (f32[3,16,16,256]{3,2,1,0:T(8,128)S(1)}, f32[3,16,16,256]{3,2,1,0:T(8,128)S(1)}, f32[3,256,512]{2,1,0:T(8,128)S(1)}, f32[3,256,512]{2,1,0:T(8,128)S(1)}) custom-call(f32[3,16,16,256]{3,2,1,0:T(8,128)} %e_in.1, f32[3,16,16,256]{3,2,1,0:T(8,128)} %h_in.1, f32[3,256,512]{2,1,0:T(8,128)} %bitcast.8, f32[3,256,512]{2,1,0:T(8,128)} %bitcast.9, ...), custom_call_target="tpu_custom_call" | custom-call | tf_op jit(solution)/shard_map/yee_gas/pallas_call | solution.py:470
  80.1 2.2 %finish.1 = (f32[3,16,16,256]{3,2,1,0:T(8,128)}, f32[3,16,16,256]{3,2,1,0:T(8,128)}, f32[3,256,512]{2,1,0:T(8,128)}, f32[3,256,512]{2,1,0:T(8,128)}) custom-call(f32[3,16,16,256]{3,2,1,0:T(8,128)S(1)} %get-tuple-element.12.refs_0_, f32[3,16,16,256]{3,2,1,0:T(8,128)S(1)} %get-tuple-element.13.refs_1_, f32[3,256,512]{2,1,0:T(8,128)S(1)} %get-tuple-element.14.refs_2_, ...), custom_call_target="tpu_custom_call" | custom-call | tf_op jit(solution)/shard_map/finish/pallas_call | solution.py:506

commit v5 on v4

--- a/solution.py
+++ b/solution.py
@@ -57,7 +57,8 @@
     up, down = lax.rem(gz + 1, G), lax.rem(gz + G - 1, G)
 
     def each(fn):
-        def body(dy, carry):
+        def body(turn, carry):
+            dy = lax.rem(turn + 1, 4)
             for dz in (2, 1, 3, 0):
                 def one(dz=dz):
                     fn(dz * 4 + dy, lax.rem(zh + dz, 4) * 4 + lax.rem(y + dy, 4))

time: 82.4 us -> 81.3 us (0.987)
  Pallas kernels: 81.7 us -> 80.3 us
    pallas_call x1, Pallas kernels: 79.4 us -> 78.1 us  [on_device(): pl.pallas_call(kernel, out_shape=[pltpu.VMEM(r.shape, r.dtype) for r in r...]
where the time goes in v5:
time: 81.3 us; the launch traced here: 80.9 us
  Pallas kernels  80.3 us (99%)
    pallas_call x1, Pallas kernels, on_device(): pl.pallas_call(kernel, out_shape=[pltpu.VMEM(r.shape, r.dtype) for r in r...  78.1 us
    pallas_call x1, Pallas kernels, on_device(): pl.pallas_call(finish, out_shape=results, in_specs=[pl.BlockSpec(memory_s...  2.22 us

profile of v5, /device:TPU:7, one launch (start us, length us, event | category | flops | bytes accessed | tf_op | source)
XLA Modules:
  0.0 80.9 jit_solution(8701255712308295576)
XLA Ops:
  0.6 78.1 %yee_gas.1 = (f32[3,16,16,256]{3,2,1,0:T(8,128)S(1)}, f32[3,16,16,256]{3,2,1,0:T(8,128)S(1)}, f32[3,256,512]{2,1,0:T(8,128)S(1)}, f32[3,256,512]{2,1,0:T(8,128)S(1)}) custom-call(f32[3,16,16,256]{3,2,1,0:T(8,128)} %e_in.1, f32[3,16,16,256]{3,2,1,0:T(8,128)} %h_in.1, f32[3,256,512]{2,1,0:T(8,128)} %bitcast.8, f32[3,256,512]{2,1,0:T(8,128)} %bitcast.9, ...), custom_call_target="tpu_custom_call" | custom-call | tf_op jit(solution)/shard_map/yee_gas/pallas_call | solution.py:471
  78.7 2.2 %finish.1 = (f32[3,16,16,256]{3,2,1,0:T(8,128)}, f32[3,16,16,256]{3,2,1,0:T(8,128)}, f32[3,256,512]{2,1,0:T(8,128)}, f32[3,256,512]{2,1,0:T(8,128)}) custom-call(f32[3,16,16,256]{3,2,1,0:T(8,128)S(1)} %get-tuple-element.12.refs_0_, f32[3,16,16,256]{3,2,1,0:T(8,128)S(1)} %get-tuple-element.13.refs_1_, f32[3,256,512]{2,1,0:T(8,128)S(1)} %get-tuple-element.14.refs_2_, ...), custom_call_target="tpu_custom_call" | custom-call | tf_op jit(solution)/shard_map/finish/pallas_call | solution.py:507
